TPU v7x, 32 devices: a whole 2x2x4 slice. The times are simulated.
32 devices in a mesh: grp: 2 (over y), rows: 8 (over z, x), diam: 2 (over core).
Axes of the slice: x: 2, y: 2, z: 4, core: 2. Of those that a mesh axis runs over, the one named last changes fastest.
Arguments:
- phi: bfloat16 [8192, 3200], P('rows', 'diam'), may hold values from -0.4375 to 0.4375
- loads: bfloat16 [8192, 512], P('rows'), may hold values from -1 to 1
- harm_diam: int32 [16], replicated, may hold values from 0 to 15
- mistuning: float32 [3200, 3200], P('diam', 'rows'), may hold values from -0.109375 to 0.109375
- dyn_diag: float32 [6400], P('grp'), parts along dimension 0, may hold values from 0.8 to 3
- blade_order: int32 [16], replicated, may hold values from 0 to 15, each once
Outputs:
- blades: bfloat16 [16, 64, 8192], P('diam', 'grp', 'rows'), parts along dimension 1
There are 2 independent parts, one for each index of `grp`. A program takes and returns all parts, laid end to end along the dimension named above; an argument that names none is the same for every part. Nothing has to cross between parts.
Inputs may be any that keep to these rules, and one draw needn't show every extreme that they name: `blade_order`: each blade once.
All inputs are finite; a program needn't handle non-finite values.
Results may differ from a plain program's by a relative error of at most 0.013.
Values may be sent and summed in bfloat16 or wider, within the bound.
No kernel may reach another device: no remote copies, remote signals or barrier semaphores. Data moves between devices by JAX's collectives and lax.ppermute only.
A program may use at most 64 MiB of HBM per device.

v0:
```python
import math
import jax
import jax.numpy as jnp
from jax import lax
from jax.sharding import PartitionSpec as P

NBLADE = 16
MODES = 200
NHARM = 16
ITERS = 4
SWAP = [(0, 1), (1, 0)]
F32 = jnp.float32
BF16 = jnp.bfloat16


def cyclic_rows(blade_order):
    count = NBLADE
    blade_pos = jnp.arange(count).astype(jnp.float32)[:, None]
    harmonic = jnp.arange(count)[None, :]
    half_count = count // 2
    wave = jnp.where(harmonic > half_count, harmonic - half_count, harmonic).astype(jnp.float32)
    angle = 2.0 * math.pi * wave * blade_pos / count
    scale = jnp.where(
        (harmonic == 0) | (harmonic == half_count), 1.0 / math.sqrt(count), math.sqrt(2.0 / count)
    )
    cyclic_tab = jnp.where(harmonic > half_count, jnp.sin(angle), jnp.cos(angle)) * scale
    onehot = (blade_order[:, None] == jnp.arange(count)[None, :]).astype(jnp.float32)
    return jnp.dot(onehot, cyclic_tab, precision=lax.Precision.HIGHEST)


def general_plan(phi, loads, harm_diam, mistuning, dyn_diag, blade_order):
    rows_dev = phi.shape[0]
    half_modes = phi.shape[1]
    local_diam = half_modes // MODES
    columns = loads.shape[1] // NHARM
    col_width = mistuning.shape[1]
    diam_index = lax.axis_index("diam")
    row_index = lax.axis_index("rows")
    first_diam = diam_index * local_diam
    diam_ids = first_diam + jnp.arange(local_diam, dtype=jnp.int32)
    select = (harm_diam[:, None] == diam_ids[None, :]).astype(jnp.bfloat16)
    combined = jnp.einsum(
        "rkc,kh->rhc",
        loads.reshape(rows_dev, NHARM, columns),
        select,
        preferred_element_type=jnp.float32,
    ).astype(jnp.bfloat16)
    shapes = phi.reshape(rows_dev, local_diam, MODES)
    force_part = jnp.einsum(
        "rhm,rhc->hmc", shapes, combined, preferred_element_type=jnp.float32
    ).reshape(half_modes, columns)
    half_start = diam_index * half_modes
    dyn_half = lax.dynamic_slice_in_dim(dyn_diag, half_start, half_modes, 0)[:, None]

    def row_total(partial_term):
        return lax.psum(partial_term, "rows")

    force_half = row_total(force_part)
    amp_half = force_half / dyn_half
    for sweep in range(ITERS):
        full_amp = lax.all_gather(amp_half, "diam", axis=0, tiled=True)
        col_part = lax.dynamic_slice_in_dim(full_amp, row_index * col_width, col_width, 0)
        amp_half = (
            force_half
            - row_total(
                jnp.dot(
                    mistuning,
                    col_part,
                    precision=lax.Precision.HIGHEST,
                    preferred_element_type=jnp.float32,
                )
            )
        ) / dyn_half
    amp_low = amp_half.astype(jnp.bfloat16).reshape(local_diam, MODES, columns)
    sector = jnp.einsum("rhm,hmc->hcr", shapes, amp_low, preferred_element_type=jnp.float32).astype(
        jnp.bfloat16
    )
    table = cyclic_rows(blade_order)
    table_cols = lax.dynamic_slice_in_dim(table, first_diam, local_diam, 1)
    partial_value = jnp.einsum(
        "sh,hcr->scr", table_cols, sector.astype(jnp.float32), precision=lax.Precision.HIGHEST
    )
    blades = lax.psum_scatter(
        partial_value.astype(jnp.bfloat16), "diam", scatter_dimension=0, tiled=True
    )
    return blades


def by_parity(arr, parity):
    pairs = arr.reshape((arr.shape[0] // 2, 2) + arr.shape[1:])
    return jnp.where(parity == 0, pairs[:, 0], pairs[:, 1])


def chunk_plan(phi, loads, harm_diam, mistuning, dyn_diag, blade_order):
    rows_dev, half_modes = phi.shape
    local_diam = half_modes // MODES
    columns = loads.shape[1] // NHARM
    core = lax.axis_index("diam")
    own_diam = 2 * lax.axis_index("rows") + core
    first_diam = core * local_diam

    def other_core(value):
        return lax.ppermute(value, "diam", SWAP)

    def in_half_order(own, received):
        return jnp.where(
            core == 0, jnp.concatenate([own, received]), jnp.concatenate([received, own])
        )

    shapes = phi.T.reshape(local_diam, MODES, rows_dev)
    shapes_received = other_core(shapes)
    stiff = mistuning.T.reshape(2 * MODES, local_diam, MODES).transpose(1, 0, 2).astype(BF16)
    coupling = in_half_order(by_parity(stiff, core), other_core(by_parity(stiff, 1 - core)))
    coupling_own = jnp.where(core == 0, coupling[:, :MODES], coupling[:, MODES:])
    coupling_other = jnp.where(core == 0, coupling[:, MODES:], coupling[:, :MODES])
    diam_ids = first_diam + jnp.arange(local_diam, dtype=jnp.int32)
    select = (harm_diam[None, :] == diam_ids[:, None]).astype(BF16)
    spread = jnp.einsum("hk,cd->hckd", select, jnp.eye(columns, dtype=BF16)).reshape(
        local_diam * columns, NHARM * columns
    )
    combined = (
        jnp.einsum("ak,rk->ar", spread, loads, preferred_element_type=F32)
        .astype(BF16)
        .reshape(local_diam, columns, rows_dev)
    )
    force_part = jnp.einsum("hcr,hmr->hcm", combined, shapes, preferred_element_type=F32).astype(
        BF16
    )
    force_slots = in_half_order(
        by_parity(force_part, core), other_core(by_parity(force_part, 1 - core))
    )

    def row_total(slots):
        got = lax.all_to_all(slots, "rows", 0, 0, tiled=True)
        return jnp.sum(got.astype(F32), axis=0)

    dyn_own = lax.dynamic_slice_in_dim(dyn_diag, own_diam * MODES, MODES, 0)[None, :]
    force = row_total(force_slots)
    amp = force / dyn_own
    for sweep in range(ITERS):
        amp_low = amp.astype(BF16)
        amp_other = other_core(amp_low)
        part = jnp.einsum("cj,sjm->scm", amp_low, coupling_own, preferred_element_type=F32)
        part = part + jnp.einsum(
            "cj,sjm->scm", amp_other, coupling_other, preferred_element_type=F32
        )
        amp = (force - row_total(part.astype(BF16))) / dyn_own
    amp_low = amp.astype(BF16)
    same = lax.all_to_all(
        jnp.broadcast_to(amp_low[None], (local_diam,) + amp_low.shape), "rows", 0, 0, tiled=True
    )
    crossed = other_core(same)
    even = jnp.where(core == 0, same, crossed)
    odd = jnp.where(core == 0, crossed, same)
    amps = jnp.stack([even, odd], axis=1).reshape(NBLADE, columns, MODES)
    table = lax.dynamic_slice_in_dim(cyclic_rows(blade_order), first_diam, local_diam, 0)
    weights = (table.T[:, :, None, None] * amps.astype(F32)[:, None]).astype(BF16)
    weights = weights.reshape(2, local_diam, local_diam * columns, MODES)
    mine = jnp.where(core == 0, weights[0], weights[1])
    theirs = jnp.where(core == 0, weights[1], weights[0])
    blades = jnp.einsum("ham,hmr->ar", mine, shapes, preferred_element_type=F32) + jnp.einsum(
        "ham,hmr->ar", theirs, shapes_received, preferred_element_type=F32
    )
    return blades.astype(BF16).reshape(local_diam, columns, rows_dev)


def solution(mesh):
    placed = (P("rows", "diam"), P("rows", None), P(), P("diam", "rows"), P("grp"), P())
    one_each = mesh.shape["rows"] * 2 == NBLADE and mesh.shape["diam"] == 2
    return jax.shard_map(
        chunk_plan if one_each else general_plan,
        mesh=mesh,
        in_specs=placed,
        out_specs=P("diam", "grp", "rows"),
        check_vma=False,
    )
```

profile of v0, /device:TPU:0, one launch (start us, length us, event | category | flops | bytes accessed | tf_op | source)
XLA Modules:
  0.0 101.7 jit_solution(17523021051338704440)
XLA Ops:
  0.0 0.8 compare_convert_fusion
  0.8 0.1 multiply_bitcast_fusion
  1.0 1.0 reshape.109
  2.0 0.5 convolution_convert_fusion
  2.5 3.2 %convolution_convert_fusion.1 = bf16[8,32,200]{2,1,0:T(8,128)(2,1)S(1)} fusion(bf16[8,32,1024]{2,1,0:T(8,128)(2,1)S(1)} %bitcast.125, bf16[8,200,1024]{2,1,0:T(8,128)(2,1)} %bitcast.122), kind=kOutput, calls=%fused_computation.8 | convolution fusion | flops 104908800 | bytes 3903488 | tf_op jit(solution)/shard_map/hcr,hmr->hcm/dot_general | solution.py:126
  5.7 0.5 collective-permute-start
  6.2 0.1 convert_bitcast_fusion
  6.4 3.5 %convert_element_type.117 = bf16[400,8,200]{2,1,0:T(8,128)(2,1)} reshape(bf16[400,1600]{1,0:T(8,128)(2,1)S(1)} %convert_bitcast_fusion) | data formatting | bytes 2560000 | tf_op jit(solution)/shard_map/convert_element_type | solution.py:112
  9.9 1.8 %copy.23 = bf16[8,400,200]{2,1,0:T(8,128)(2,1)S(1)} copy(bf16[8,400,200]{2,0,1:T(8,128)(2,1)} %bitcast.121) | data formatting | bytes 2560000 | tf_op jit(solution)/shard_map/convert_element_type | solution.py:112
  11.6 1.0 select_bitcast_fusion
  12.7 0.8 dynamic_slice.7
  13.4 0.7 maximum_select_fusion.1
  14.1 7.3 %all-to-all-start = ((bf16[8,32,200]{2,1,0:T(8,128)(2,1)}), bf16[8,32,200]{2,1,0:T(8,128)(2,1)}, u32[]{:S(2)}, u32[]{:S(2)}) async-start(bf16[8,32,200]{2,1,0:T(8,128)(2,1)} %maximum_select_fusion.1), calls=%async_computation | async-start | bytes 262144 | tf_op jit(solution)/shard_map/all_to_all | solution.py:134
  21.4 0.1 fusion.2
  21.5 7.4 %all-to-all-done = bf16[8,32,200]{2,1,0:T(8,128)(2,1)} async-done(((bf16[8,32,200]{2,1,0:T(8,128)(2,1)}), bf16[8,32,200]{2,1,0:T(8,128)(2,1)}, u32[]{:S(2)}, u32[]{:S(2)}) %all-to-all-start) | async-done | bytes 102432 | tf_op jit(solution)/shard_map/all_to_all | solution.py:134
  28.9 0.9 convert_reduce_fusion.4
  29.9 2.0 %maximum_select_fusion = bf16[8,400,200]{2,1,0:T(8,128)(2,1)S(1)} fusion(bf16[4,400,200]{2,1,0:T(8,128)(2,1)} %collective-permute-done.1, bf16[4,400,200]{2,1,0:T(8,128)(2,1)S(1)} %fusion.2, pred[]{:T(512)S(6)} %eq.61), kind=kLoop, calls=%fused_computation.1 | loop fusion | flops 1920000 | bytes 2560001 | tf_op jit(solution)/shard_map/jit(_where)/select_n | solution.py:106
  31.9 0.1 broadcast_select_fusion.3
  32.0 0.2 fusion.25
  32.2 0.3 fusion.3
  32.5 10.3 %all_to_all.30 = bf16[8,32,200]{2,1,0:T(8,128)(2,1)S(1)} all-to-all(bf16[8,32,200]{2,1,0:T(8,128)(2,1)S(1)} %fusion.3), channel_id=1, replica_groups=mesh['grp'=2,'rows'=8,'diam'=2] {'rows'}, dimensions={0} | all-to-all | bytes 204800 | tf_op jit(solution)/shard_map/all_to_all | solution.py:134
  42.9 0.1 collective-permute-start.3
  43.0 1.2 %collective-permute-done.3 = bf16[32,200]{1,0:T(8,128)(2,1)S(1)} collective-permute-done((bf16[32,200]{1,0:T(8,128)(2,1)S(1)}, bf16[32,200]{1,0:T(8,128)(2,1)S(1)}, u32[]{:S(2)}, u32[]{:S(2)}) %collective-permute-start.3) | collective-permute-done | bytes 12832 | tf_op jit(solution)/shard_map/ppermute | solution.py:103
  44.1 0.2 fusion.19
  44.4 0.3 fusion.4
  44.6 10.0 %all_to_all.31 = bf16[8,32,200]{2,1,0:T(8,128)(2,1)S(1)} all-to-all(bf16[8,32,200]{2,1,0:T(8,128)(2,1)S(1)} %fusion.4), channel_id=1, replica_groups=mesh['grp'=2,'rows'=8,'diam'=2] {'rows'}, dimensions={0} | all-to-all | bytes 204800 | tf_op jit(solution)/shard_map/all_to_all | solution.py:134
  54.8 1.2 %collective-permute-done.4 = bf16[32,200]{1,0:T(8,128)(2,1)S(1)} collective-permute-done((bf16[32,200]{1,0:T(8,128)(2,1)S(1)}, bf16[32,200]{1,0:T(8,128)(2,1)S(1)}, u32[]{:S(2)}, u32[]{:S(2)}) %collective-permute-start.4) | collective-permute-done | bytes 12832 | tf_op jit(solution)/shard_map/ppermute | solution.py:103
  55.9 0.2 fusion.13
  56.2 0.9 fusion.5
  57.1 3.5 %all-to-all-start.3 = ((bf16[8,32,200]{2,1,0:T(8,128)(2,1)}), bf16[8,32,200]{2,1,0:T(8,128)(2,1)S(1)}, u32[]{:S(2)}, u32[]{:S(2)}) async-start(bf16[8,32,200]{2,1,0:T(8,128)(2,1)} %fusion.5), calls=%async_computation.3 | async-start | bytes 262144 | tf_op jit(solution)/shard_map/all_to_all | solution.py:134
  60.6 0.2 collective-permute-start.7
  60.8 7.3 %all-to-all-done.3 = bf16[8,32,200]{2,1,0:T(8,128)(2,1)S(1)} async-done(((bf16[8,32,200]{2,1,0:T(8,128)(2,1)}), bf16[8,32,200]{2,1,0:T(8,128)(2,1)S(1)}, u32[]{:S(2)}, u32[]{:S(2)}) %all-to-all-start.3) | async-done | bytes 102432 | tf_op jit(solution)/shard_map/all_to_all | solution.py:134
  68.3 1.2 %collective-permute-done.5 = bf16[32,200]{1,0:T(8,128)(2,1)S(1)} collective-permute-done((bf16[32,200]{1,0:T(8,128)(2,1)S(1)}, bf16[32,200]{1,0:T(8,128)(2,1)S(1)}, u32[]{:S(2)}, u32[]{:S(2)}) %collective-permute-start.5) | collective-permute-done | bytes 12832 | tf_op jit(solution)/shard_map/ppermute | solution.py:103
  69.4 0.2 fusion.7
  69.7 0.9 fusion.6
  70.6 3.4 %all-to-all-start.4 = ((bf16[8,32,200]{2,1,0:T(8,128)(2,1)}), bf16[8,32,200]{2,1,0:T(8,128)(2,1)S(1)}, u32[]{:S(2)}, u32[]{:S(2)}) async-start(bf16[8,32,200]{2,1,0:T(8,128)(2,1)} %fusion.6), calls=%async_computation.4 | async-start | bytes 262144 | tf_op jit(solution)/shard_map/all_to_all | solution.py:134
  74.0 7.5 %all-to-all-done.4 = bf16[8,32,200]{2,1,0:T(8,128)(2,1)S(1)} async-done(((bf16[8,32,200]{2,1,0:T(8,128)(2,1)}), bf16[8,32,200]{2,1,0:T(8,128)(2,1)S(1)}, u32[]{:S(2)}, u32[]{:S(2)}) %all-to-all-start.4) | async-done | bytes 102432 | tf_op jit(solution)/shard_map/all_to_all | solution.py:134
  81.5 0.7 broadcast_in_dim.21
  82.2 3.4 %all-to-all-start.5 = ((bf16[8,32,200]{2,1,0:T(8,128)(2,1)}), bf16[8,32,200]{2,1,0:T(8,128)(2,1)S(1)}, u32[]{:S(2)}, u32[]{:S(2)}) async-start(bf16[8,32,200]{2,1,0:T(8,128)(2,1)} %broadcast_in_dim.21), calls=%async_computation.5 | async-start | bytes 262144 | tf_op jit(solution)/shard_map/all_to_all | solution.py:149
  85.6 0.2 fusion.32
  85.8 7.0 %all-to-all-done.5 = bf16[8,32,200]{2,1,0:T(8,128)(2,1)S(1)} async-done(((bf16[8,32,200]{2,1,0:T(8,128)(2,1)}), bf16[8,32,200]{2,1,0:T(8,128)(2,1)S(1)}, u32[]{:S(2)}, u32[]{:S(2)}) %all-to-all-start.5) | async-done | bytes 102432 | tf_op jit(solution)/shard_map/all_to_all | solution.py:149
  92.9 0.1 copy.20
  92.9 1.3 %collective-permute-done.6 = bf16[8,32,200]{2,1,0:T(8,128)(2,1)S(1)} collective-permute-done((bf16[8,32,200]{2,1,0:T(8,128)(2,1)S(1)}, bf16[8,32,200]{2,1,0:T(8,128)(2,1)S(1)}, u32[]{:S(2)}, u32[]{:S(2)}) %collective-permute-start.6) | collective-permute-done | bytes 102432 | tf_op jit(solution)/shard_map/ppermute | solution.py:103
  94.4 0.3 multiply_convert_fusion
  94.7 0.1 broadcast_select_fusion
  94.9 1.8 %copy-done.1 = bf16[1024,1600]{0,1:T(8,128)(2,1)S(1)} copy-done((bf16[1024,1600]{0,1:T(8,128)(2,1)S(1)}, bf16[1024,1600]{0,1:T(8,128)(2,1)}, u32[]{:S(2)}) %copy-start.1) | copy-done | bytes 3276824
  96.7 1.2 %convolution_bitcast_fusion.1 = f32[256,1024]{1,0:T(8,128)S(1)} fusion(bf16[8,256,200]{2,1,0:T(8,128)(2,1)S(1)} %bitcast.127, bf16[8,200,1024]{2,1,0:T(8,128)(2,1)S(1)} %bitcast.124), kind=kOutput, calls=%fused_computation.3 | convolution fusion | flops 838860800 | bytes 5144576 | tf_op jit(solution)/shard_map/ham,hmr->ar/dot_general | solution.py:161
  97.8 3.9 %fusion.1 = bf16[256,1024]{1,0:T(8,128)(2,1)} fusion(f32[256,1024]{1,0:T(8,128)S(1)} %convolution_bitcast_fusion.1, bf16[8,256,200]{2,1,0:T(8,128)(2,1)S(1)} %bitcast.126, bf16[8,200,1024]{2,1,0:T(8,128)(2,1)} %collective-permute-done.7), kind=kOutput, calls=%fused_computation.7 | convolution fusion | flops 839385088 | bytes 5668864 | tf_op jit(solution)/shard_map/ham,hmr->ar/dot_general | solution.py:161
  (35 shorter events, 0.6 us)
Async XLA Ops:
  0.0 2.0 %copy-start = (bf16[1024,512]{1,0:T(8,128)(2,1)S(1)}, bf16[1024,512]{1,0:T(8,128)(2,1)}, u32[]{:S(2)}) copy-start(bf16[1024,512]{1,0:T(8,128)(2,1)} %param.7) | copy-start | bytes 3145732
  2.5 3.8 %copy-start.2 = (f32[1600,400]{0,1:T(8,128)S(1)}, f32[1600,400]{0,1:T(8,128)}, u32[]{:S(2)}) copy-start(f32[1600,400]{0,1:T(8,128)} %param.9) | copy-start | bytes 7680004
  5.7 7.7 %collective-permute-start = (bf16[4,32,200]{2,1,0:T(8,128)(2,1)S(1)}, bf16[4,32,200]{2,1,0:T(8,128)(2,1)S(1)}, u32[]{:S(2)}, u32[]{:S(2)}) collective-permute-start(bf16[4,32,200]{2,1,0:T(8,128)(2,1)S(1)} %get-tuple-element.12), channel_id=1, source_target_pairs={{0,1},{1,0},{2,3},{3,2},{4,5},{5,4},{6,7},{7,6},{8,9},{9,8},{10,11... | collective-permute-start | bytes 153608 | tf_op jit(solution)/shard_map/ppermute | solution.py:103
  12.6 17.3 %collective-permute-start.1 = (bf16[4,400,200]{2,1,0:T(8,128)(2,1)}, bf16[4,400,200]{2,1,0:T(8,128)(2,1)}, u32[]{:S(2)}, u32[]{:S(2)}) collective-permute-start(bf16[4,400,200]{2,1,0:T(8,128)(2,1)} %select_bitcast_fusion), channel_id=1, source_target_pairs={{0,1},{1,0},{2,3},{3,2},{4,5},{5,4},{6,7},{7,6},{8,9},{9,8},{10,11... | collective-permute-start | bytes 1920008 | tf_op jit(solution)/shard_map/ppermute | solution.py:103
  14.1 14.7 %all-to-all-start = ((bf16[8,32,200]{2,1,0:T(8,128)(2,1)}), bf16[8,32,200]{2,1,0:T(8,128)(2,1)}, u32[]{:S(2)}, u32[]{:S(2)}) async-start(bf16[8,32,200]{2,1,0:T(8,128)(2,1)} %maximum_select_fusion.1), calls=%async_computation | async-start | bytes 262144 | tf_op jit(solution)/shard_map/all_to_all | solution.py:134
  29.8 2.2 %collective-permute-start.2 = (bf16[32,200]{1,0:T(8,128)(2,1)S(1)}, bf16[32,200]{1,0:T(8,128)(2,1)S(1)}, u32[]{:S(2)}, u32[]{:S(2)}) collective-permute-start(bf16[32,200]{1,0:T(8,128)(2,1)S(1)} %divide_convert_fusion.4), channel_id=1, source_target_pairs={{0,1},{1,0},{2,3},{3,2},{4,5},{5,4},{6,7},{7,6},{8,9},{9,8},{10,11... | collective-permute-start | bytes 38408 | tf_op jit(solution)/shard_map/ppermute | solution.py:103
  42.9 1.2 %collective-permute-start.3 = (bf16[32,200]{1,0:T(8,128)(2,1)S(1)}, bf16[32,200]{1,0:T(8,128)(2,1)S(1)}, u32[]{:S(2)}, u32[]{:S(2)}) collective-permute-start(bf16[32,200]{1,0:T(8,128)(2,1)S(1)} %divide_convert_fusion.3), channel_id=1, source_target_pairs={{0,1},{1,0},{2,3},{3,2},{4,5},{5,4},{6,7},{7,6},{8,9},{9,8},{10,11... | collective-permute-start | bytes 38408 | tf_op jit(solution)/shard_map/ppermute | solution.py:103
  54.7 1.2 %collective-permute-start.4 = (bf16[32,200]{1,0:T(8,128)(2,1)S(1)}, bf16[32,200]{1,0:T(8,128)(2,1)S(1)}, u32[]{:S(2)}, u32[]{:S(2)}) collective-permute-start(bf16[32,200]{1,0:T(8,128)(2,1)S(1)} %divide_convert_fusion.2), channel_id=1, source_target_pairs={{0,1},{1,0},{2,3},{3,2},{4,5},{5,4},{6,7},{7,6},{8,9},{9,8},{10,11... | collective-permute-start | bytes 38408 | tf_op jit(solution)/shard_map/ppermute | solution.py:103
  57.1 28.5 %copy-start.3 = (s32[16]{0:T(128)S(1)}, s32[16]{0:T(128)}, u32[]{:S(2)}) copy-start(s32[16]{0:T(128)} %param.11) | copy-start | bytes 196
  57.1 11.0 %all-to-all-start.3 = ((bf16[8,32,200]{2,1,0:T(8,128)(2,1)}), bf16[8,32,200]{2,1,0:T(8,128)(2,1)S(1)}, u32[]{:S(2)}, u32[]{:S(2)}) async-start(bf16[8,32,200]{2,1,0:T(8,128)(2,1)} %fusion.5), calls=%async_computation.3 | async-start | bytes 262144 | tf_op jit(solution)/shard_map/all_to_all | solution.py:134
  60.6 37.2 %collective-permute-start.7 = (bf16[8,200,1024]{2,1,0:T(8,128)(2,1)}, bf16[8,200,1024]{2,1,0:T(8,128)(2,1)}, u32[]{:S(2)}, u32[]{:S(2)}) collective-permute-start(bf16[8,200,1024]{2,1,0:T(8,128)(2,1)} %bitcast.123), channel_id=1, source_target_pairs={{0,1},{1,0},{2,3},{3,2},{4,5},{5,4},{6,7},{7,6},{8,9},{9,8},{10,11... | collective-permute-start | bytes 9830408 | tf_op jit(solution)/shard_map/ppermute | solution.py:103
  68.2 1.2 %collective-permute-start.5 = (bf16[32,200]{1,0:T(8,128)(2,1)S(1)}, bf16[32,200]{1,0:T(8,128)(2,1)S(1)}, u32[]{:S(2)}, u32[]{:S(2)}) collective-permute-start(bf16[32,200]{1,0:T(8,128)(2,1)S(1)} %divide_convert_fusion.1), channel_id=1, source_target_pairs={{0,1},{1,0},{2,3},{3,2},{4,5},{5,4},{6,7},{7,6},{8,9},{9,8},{10,11... | collective-permute-start | bytes 38408 | tf_op jit(solution)/shard_map/ppermute | solution.py:103
  70.6 10.9 %all-to-all-start.4 = ((bf16[8,32,200]{2,1,0:T(8,128)(2,1)}), bf16[8,32,200]{2,1,0:T(8,128)(2,1)S(1)}, u32[]{:S(2)}, u32[]{:S(2)}) async-start(bf16[8,32,200]{2,1,0:T(8,128)(2,1)} %fusion.6), calls=%async_computation.4 | async-start | bytes 262144 | tf_op jit(solution)/shard_map/all_to_all | solution.py:134
  82.2 10.7 %all-to-all-start.5 = ((bf16[8,32,200]{2,1,0:T(8,128)(2,1)}), bf16[8,32,200]{2,1,0:T(8,128)(2,1)S(1)}, u32[]{:S(2)}, u32[]{:S(2)}) async-start(bf16[8,32,200]{2,1,0:T(8,128)(2,1)} %broadcast_in_dim.21), calls=%async_computation.5 | async-start | bytes 262144 | tf_op jit(solution)/shard_map/all_to_all | solution.py:149
  92.9 1.3 %collective-permute-start.6 = (bf16[8,32,200]{2,1,0:T(8,128)(2,1)S(1)}, bf16[8,32,200]{2,1,0:T(8,128)(2,1)S(1)}, u32[]{:S(2)}, u32[]{:S(2)}) collective-permute-start(bf16[8,32,200]{2,1,0:T(8,128)(2,1)S(1)} %all-to-all-done.5), channel_id=1, source_target_pairs={{0,1},{1,0},{2,3},{3,2},{4,5},{5,4},{6,7},{7,6},{8,9},{9,8},{10,11... | collective-permute-start | bytes 307208 | tf_op jit(solution)/shard_map/ppermute | solution.py:103
  94.7 1.9 %copy-start.1 = (bf16[1024,1600]{0,1:T(8,128)(2,1)S(1)}, bf16[1024,1600]{0,1:T(8,128)(2,1)}, u32[]{:S(2)}) copy-start(bf16[1024,1600]{0,1:T(8,128)(2,1)} %param.6) | copy-start | bytes 9830404
where the time goes:
time: 102 us
  waiting for transfers between devices  34 us (33%)
  blocking collectives  20.3 us (20%)
  starting transfers between devices  18.6 us (18%)
  matrix products  12.3 us (12%)
  local copies, waits for them, and re-layouts  9.56 us (9%)
  other arithmetic  6.71 us (7%)
    all_to_all x3, waiting for transfers between devices, row_total(): got = lax.all_to_all(slots, 'rows', 0, 0, tiled=True)  22.2 us
    all_to_all x2, blocking collectives, row_total(): got = lax.all_to_all(slots, 'rows', 0, 0, tiled=True)  20.3 us
    all_to_all x3, starting transfers between devices, row_total(): got = lax.all_to_all(slots, 'rows', 0, 0, tiled=True)  14.1 us
    all_to_all x1, waiting for transfers between devices, chunk_plan(): lax.all_to_all(jnp.broadcast_to(amp_low[None], (local_diam,) + amp_low.sh...  7.03 us
    convert_element_type x2, local copies, waits for them, and re-layouts, chunk_plan(): mistuning.T.reshape(2 * MODES, local_diam, MODES).transpose(1, 0, 2)  5.26 us
    ppermute x8, waiting for transfers between devices, other_core(): return lax.ppermute(value, 'diam', SWAP)  4.78 us
    dot_general x1, matrix products, chunk_plan(): jnp.einsum('ham,hmr->ar', theirs, shapes_received, preferred_element_type...  3.91 us
    all_to_all x1, starting transfers between devices, chunk_plan(): lax.all_to_all(jnp.broadcast_to(amp_low[None], (local_diam,) + amp_low.sh...  3.37 us
  transfers between devices with their start and end apart: 12, of which 8 were waited for; matrix products, arithmetic and copies ran while one was open for 15% of the time, Pallas kernels for 0%

commit v1 on v0

--- a/solution.py
+++ b/solution.py
@@ -146,9 +146,20 @@
         )
         amp = (force - row_total(part.astype(BF16))) / dyn_own
     amp_low = amp.astype(BF16)
-    same = lax.all_to_all(
-        jnp.broadcast_to(amp_low[None], (local_diam,) + amp_low.shape), "rows", 0, 0, tiled=True
-    )
+    array = jnp.broadcast_to(amp_low[None], (local_diam,) + amp_low.shape)
+    ways, here = (lax.axis_size("rows"), lax.axis_index("rows"))
+    width = array.shape[0] // ways
+    dims = list(array.shape)
+    dims[0] = width
+    height = dims[0]
+    dims[0] = height * ways
+    full = jnp.zeros(dims, array.dtype)
+    for mask in range(ways):
+        part_2 = lax.dynamic_slice_in_dim(array, (here ^ mask) * width, width, axis=0)
+        if mask:
+            part_2 = lax.ppermute(part_2, "rows", [(d, d ^ mask) for d in range(ways)])
+        full = lax.dynamic_update_slice_in_dim(full, part_2, (here ^ mask) * height, axis=0)
+    same = full
     crossed = other_core(same)
     even = jnp.where(core == 0, same, crossed)
     odd = jnp.where(core == 0, crossed, same)

time: 102 us -> 111 us (1.088)
  starting transfers between devices: 18.6 us -> 25.3 us
  waiting for transfers between devices: 34 us -> 36.5 us
    ppermute x0 -> x7, starting transfers between devices: none -> 10.2 us  [chunk_plan(): part_2 = lax.ppermute(part_2, 'rows', [(d, d ^ mask) for d in range(ways)])]
    ppermute x0 -> x7, waiting for transfers between devices: none -> 9.51 us  [chunk_plan(): part_2 = lax.ppermute(part_2, 'rows', [(d, d ^ mask) for d in range(ways)])]
    all_to_all x1 -> x0, waiting for transfers between devices: 7.03 us -> none  [chunk_plan(): lax.all_to_all(jnp.broadcast_to(amp_low[None], (local_diam,) + amp_low.sh...]
    all_to_all x1 -> x0, starting transfers between devices: 3.37 us -> none  [chunk_plan(): lax.all_to_all(jnp.broadcast_to(amp_low[None], (local_diam,) + amp_low.sh...]
  transfers between devices with their start and end apart: 12 -> 18, of which waited for: 8 -> 10; matrix products, arithmetic and copies ran while one was open for 15% -> 13% of each run, Pallas kernels for 0% -> 0%
where the time goes in v1:
time: 111 us; the launch traced here: 110 us
  waiting for transfers between devices  36.5 us (33%)
  starting transfers between devices  25.3 us (23%)
  blocking collectives  20.3 us (18%)
  matrix products  12.3 us (11%)
  local copies, waits for them, and re-layouts  8.92 us (8%)
  other arithmetic  6.73 us (6%)
    all_to_all x3, waiting for transfers between devices, row_total(): got = lax.all_to_all(slots, 'rows', 0, 0, tiled=True)  22.2 us
    all_to_all x2, blocking collectives, row_total(): got = lax.all_to_all(slots, 'rows', 0, 0, tiled=True)  20.3 us
    all_to_all x3, starting transfers between devices, row_total(): got = lax.all_to_all(slots, 'rows', 0, 0, tiled=True)  14 us
    ppermute x7, starting transfers between devices, chunk_plan(): part_2 = lax.ppermute(part_2, 'rows', [(d, d ^ mask) for d in range(ways)])  10.2 us
    ppermute x7, waiting for transfers between devices, chunk_plan(): part_2 = lax.ppermute(part_2, 'rows', [(d, d ^ mask) for d in range(ways)])  9.51 us
    convert_element_type x2, local copies, waits for them, and re-layouts, chunk_plan(): mistuning.T.reshape(2 * MODES, local_diam, MODES).transpose(1, 0, 2)  5.25 us
    ppermute x8, waiting for transfers between devices, other_core(): return lax.ppermute(value, 'diam', SWAP)  4.78 us
    dot_general x1, matrix products, chunk_plan(): jnp.einsum('ham,hmr->ar', theirs, shapes_received, preferred_element_type...  3.92 us
  transfers between devices with their start and end apart: 18, of which 10 were waited for; matrix products, arithmetic and copies ran while one was open for 13% of the time, Pallas kernels for 0%

profile of v1, /device:TPU:0, one launch (start us, length us, event | category | flops | bytes accessed | tf_op | source)
XLA Modules:
  0.0 110.3 jit_solution(16857862192483613624)
XLA Ops:
  0.0 0.8 compare_convert_fusion
  1.0 1.0 reshape.143
  2.0 0.5 convolution_convert_fusion
  2.5 3.2 %convolution_convert_fusion.1 = bf16[8,32,200]{2,1,0:T(8,128)(2,1)S(1)} fusion(bf16[8,32,1024]{2,1,0:T(8,128)(2,1)S(1)} %bitcast.130, bf16[8,200,1024]{2,1,0:T(8,128)(2,1)} %bitcast.127), kind=kOutput, calls=%fused_computation.8 | convolution fusion | flops 104908800 | bytes 3903488 | tf_op jit(solution)/shard_map/hcr,hmr->hcm/dot_general | solution.py:126
  5.7 0.5 collective-permute-start
  6.4 3.5 %convert_element_type.120 = bf16[400,8,200]{2,1,0:T(8,128)(2,1)} reshape(bf16[400,1600]{1,0:T(8,128)(2,1)S(1)} %convert_bitcast_fusion) | data formatting | bytes 2560000 | tf_op jit(solution)/shard_map/convert_element_type | solution.py:112
  9.9 1.8 %copy.23 = bf16[8,400,200]{2,1,0:T(8,128)(2,1)S(1)} copy(bf16[8,400,200]{2,0,1:T(8,128)(2,1)} %bitcast.126) | data formatting | bytes 2560000 | tf_op jit(solution)/shard_map/convert_element_type | solution.py:112
  11.6 1.0 select_bitcast_fusion
  12.7 0.8 dynamic_slice.5
  13.4 0.7 maximum_select_fusion.1
  14.1 7.3 %all-to-all-start = ((bf16[8,32,200]{2,1,0:T(8,128)(2,1)}), bf16[8,32,200]{2,1,0:T(8,128)(2,1)}, u32[]{:S(2)}, u32[]{:S(2)}) async-start(bf16[8,32,200]{2,1,0:T(8,128)(2,1)} %maximum_select_fusion.1), calls=%async_computation | async-start | bytes 262144 | tf_op jit(solution)/shard_map/all_to_all | solution.py:134
  21.5 7.4 %all-to-all-done = bf16[8,32,200]{2,1,0:T(8,128)(2,1)} async-done(((bf16[8,32,200]{2,1,0:T(8,128)(2,1)}), bf16[8,32,200]{2,1,0:T(8,128)(2,1)}, u32[]{:S(2)}, u32[]{:S(2)}) %all-to-all-start) | async-done | bytes 102432 | tf_op jit(solution)/shard_map/all_to_all | solution.py:134
  28.9 0.9 convert_reduce_fusion.4
  29.9 2.0 %maximum_select_fusion = bf16[8,400,200]{2,1,0:T(8,128)(2,1)S(1)} fusion(bf16[4,400,200]{2,1,0:T(8,128)(2,1)} %collective-permute-done.1, bf16[4,400,200]{2,1,0:T(8,128)(2,1)S(1)} %fusion.2, pred[]{:T(512)S(6)} %eq.61), kind=kLoop, calls=%fused_computation.1 | loop fusion | flops 1920000 | bytes 2560001 | tf_op jit(solution)/shard_map/jit(_where)/select_n | solution.py:106
  32.0 0.2 fusion.26
  32.2 0.3 fusion.3
  32.5 10.3 %all_to_all.25 = bf16[8,32,200]{2,1,0:T(8,128)(2,1)S(1)} all-to-all(bf16[8,32,200]{2,1,0:T(8,128)(2,1)S(1)} %fusion.3), channel_id=1, replica_groups=mesh['grp'=2,'rows'=8,'diam'=2] {'rows'}, dimensions={0} | all-to-all | bytes 204800 | tf_op jit(solution)/shard_map/all_to_all | solution.py:134
  43.0 1.2 %collective-permute-done.3 = bf16[32,200]{1,0:T(8,128)(2,1)S(1)} collective-permute-done((bf16[32,200]{1,0:T(8,128)(2,1)S(1)}, bf16[32,200]{1,0:T(8,128)(2,1)S(1)}, u32[]{:S(2)}, u32[]{:S(2)}) %collective-permute-start.3) | collective-permute-done | bytes 12832 | tf_op jit(solution)/shard_map/ppermute | solution.py:103
  44.1 0.2 fusion.20
  44.4 0.3 fusion.4
  44.6 10.0 %all_to_all.26 = bf16[8,32,200]{2,1,0:T(8,128)(2,1)S(1)} all-to-all(bf16[8,32,200]{2,1,0:T(8,128)(2,1)S(1)} %fusion.4), channel_id=1, replica_groups=mesh['grp'=2,'rows'=8,'diam'=2] {'rows'}, dimensions={0} | all-to-all | bytes 204800 | tf_op jit(solution)/shard_map/all_to_all | solution.py:134
  54.7 1.2 %collective-permute-done.4 = bf16[32,200]{1,0:T(8,128)(2,1)S(1)} collective-permute-done((bf16[32,200]{1,0:T(8,128)(2,1)S(1)}, bf16[32,200]{1,0:T(8,128)(2,1)S(1)}, u32[]{:S(2)}, u32[]{:S(2)}) %collective-permute-start.4) | collective-permute-done | bytes 12832 | tf_op jit(solution)/shard_map/ppermute | solution.py:103
  55.9 0.2 fusion.14
  56.2 0.9 fusion.5
  57.1 3.4 %all-to-all-start.3 = ((bf16[8,32,200]{2,1,0:T(8,128)(2,1)}), bf16[8,32,200]{2,1,0:T(8,128)(2,1)S(1)}, u32[]{:S(2)}, u32[]{:S(2)}) async-start(bf16[8,32,200]{2,1,0:T(8,128)(2,1)} %fusion.5), calls=%async_computation.3 | async-start | bytes 262144 | tf_op jit(solution)/shard_map/all_to_all | solution.py:134
  60.5 0.2 collective-permute-start.14
  60.7 7.3 %all-to-all-done.3 = bf16[8,32,200]{2,1,0:T(8,128)(2,1)S(1)} async-done(((bf16[8,32,200]{2,1,0:T(8,128)(2,1)}), bf16[8,32,200]{2,1,0:T(8,128)(2,1)S(1)}, u32[]{:S(2)}, u32[]{:S(2)}) %all-to-all-start.3) | async-done | bytes 102432 | tf_op jit(solution)/shard_map/all_to_all | solution.py:134
  68.1 1.2 %collective-permute-done.5 = bf16[32,200]{1,0:T(8,128)(2,1)S(1)} collective-permute-done((bf16[32,200]{1,0:T(8,128)(2,1)S(1)}, bf16[32,200]{1,0:T(8,128)(2,1)S(1)}, u32[]{:S(2)}, u32[]{:S(2)}) %collective-permute-start.5) | collective-permute-done | bytes 12832 | tf_op jit(solution)/shard_map/ppermute | solution.py:103
  69.3 0.2 fusion.8
  69.5 0.9 fusion.6
  70.4 3.4 %all-to-all-start.4 = ((bf16[8,32,200]{2,1,0:T(8,128)(2,1)}), bf16[8,32,200]{2,1,0:T(8,128)(2,1)S(1)}, u32[]{:S(2)}, u32[]{:S(2)}) async-start(bf16[8,32,200]{2,1,0:T(8,128)(2,1)} %fusion.6), calls=%async_computation.4 | async-start | bytes 262144 | tf_op jit(solution)/shard_map/all_to_all | solution.py:134
  73.9 7.5 %all-to-all-done.4 = bf16[8,32,200]{2,1,0:T(8,128)(2,1)S(1)} async-done(((bf16[8,32,200]{2,1,0:T(8,128)(2,1)}), bf16[8,32,200]{2,1,0:T(8,128)(2,1)S(1)}, u32[]{:S(2)}, u32[]{:S(2)}) %all-to-all-start.4) | async-done | bytes 102432 | tf_op jit(solution)/shard_map/all_to_all | solution.py:134
  81.4 0.3 collective-permute-start.6
  81.8 0.2 fusion.33
  82.0 1.7 %collective-permute-start.11 = (bf16[1,32,200]{2,1,0:T(8,128)(2,1)S(1)}, bf16[1,32,200]{2,1,0:T(8,128)(2,1)S(1)}, u32[]{:S(2)}, u32[]{:S(2)}) collective-permute-start(bf16[1,32,200]{2,1,0:T(8,128)(2,1)S(1)} %get-tuple-element.6), channel_id=1, source_target_pairs={{0,12},{2,14},{4,8},{6,10},{8,4},{10,6},{12,0},{14,2},{1,13},{3,15... | collective-permute-start | bytes 38408 | tf_op jit(solution)/shard_map/ppermute | solution.py:160
  83.7 0.9 collective-permute-start.10
  84.6 2.0 %collective-permute-start.9 = (bf16[1,32,200]{2,1,0:T(8,128)(2,1)S(1)}, bf16[1,32,200]{2,1,0:T(8,128)(2,1)S(1)}, u32[]{:S(2)}, u32[]{:S(2)}) collective-permute-start(bf16[1,32,200]{2,1,0:T(8,128)(2,1)S(1)} %get-tuple-element.6), channel_id=1, source_target_pairs={{0,8},{2,10},{4,12},{6,14},{8,0},{10,2},{12,4},{14,6},{1,9},{3,11}... | collective-permute-start | bytes 38408 | tf_op jit(solution)/shard_map/ppermute | solution.py:160
  86.6 1.0 collective-permute-start.7
  87.6 2.7 %collective-permute-done.7 = bf16[1,32,200]{2,1,0:T(8,128)(2,1)S(1)} collective-permute-done((bf16[1,32,200]{2,1,0:T(8,128)(2,1)S(1)}, bf16[1,32,200]{2,1,0:T(8,128)(2,1)S(1)}, u32[]{:S(2)}, u32[]{:S(2)}) %collective-permute-start.7) | collective-permute-done | bytes 12832 | tf_op jit(solution)/shard_map/ppermute | solution.py:160
  90.3 1.1 %collective-permute-start.8 = (bf16[1,32,200]{2,1,0:T(8,128)(2,1)S(1)}, bf16[1,32,200]{2,1,0:T(8,128)(2,1)S(1)}, u32[]{:S(2)}, u32[]{:S(2)}) collective-permute-start(bf16[1,32,200]{2,1,0:T(8,128)(2,1)S(1)} %get-tuple-element.6), channel_id=1, source_target_pairs={{0,6},{2,4},{4,2},{6,0},{8,14},{10,12},{12,10},{14,8},{1,7},{3,5},... | collective-permute-start | bytes 38408 | tf_op jit(solution)/shard_map/ppermute | solution.py:160
  91.5 3.5 %collective-permute-done.8 = bf16[1,32,200]{2,1,0:T(8,128)(2,1)S(1)} collective-permute-done((bf16[1,32,200]{2,1,0:T(8,128)(2,1)S(1)}, bf16[1,32,200]{2,1,0:T(8,128)(2,1)S(1)}, u32[]{:S(2)}, u32[]{:S(2)}) %collective-permute-start.8) | collective-permute-done | bytes 12832 | tf_op jit(solution)/shard_map/ppermute | solution.py:160
  95.0 3.1 %collective-permute-start.12 = (bf16[1,32,200]{2,1,0:T(8,128)(2,1)S(1)}, bf16[1,32,200]{2,1,0:T(8,128)(2,1)S(1)}, u32[]{:S(2)}, u32[]{:S(2)}) collective-permute-start(bf16[1,32,200]{2,1,0:T(8,128)(2,1)S(1)} %get-tuple-element.6), channel_id=1, source_target_pairs={{0,14},{2,12},{4,10},{6,8},{8,6},{10,4},{12,2},{14,0},{1,15},{3,13... | collective-permute-start | bytes 38408 | tf_op jit(solution)/shard_map/ppermute | solution.py:160
  98.1 3.3 %collective-permute-done.12 = bf16[1,32,200]{2,1,0:T(8,128)(2,1)S(1)} collective-permute-done((bf16[1,32,200]{2,1,0:T(8,128)(2,1)S(1)}, bf16[1,32,200]{2,1,0:T(8,128)(2,1)S(1)}, u32[]{:S(2)}, u32[]{:S(2)}) %collective-permute-start.12) | collective-permute-done | bytes 12832 | tf_op jit(solution)/shard_map/ppermute | solution.py:160
  101.5 1.3 %collective-permute-done.13 = bf16[8,32,200]{2,1,0:T(8,128)(2,1)S(1)} collective-permute-done((bf16[8,32,200]{2,1,0:T(8,128)(2,1)S(1)}, bf16[8,32,200]{2,1,0:T(8,128)(2,1)S(1)}, u32[]{:S(2)}, u32[]{:S(2)}) %collective-permute-start.13) | collective-permute-done | bytes 102432 | tf_op jit(solution)/shard_map/ppermute | solution.py:103
  102.9 0.4 multiply_convert_fusion
  103.4 1.8 %copy-done.1 = bf16[1024,1600]{0,1:T(8,128)(2,1)S(1)} copy-done((bf16[1024,1600]{0,1:T(8,128)(2,1)S(1)}, bf16[1024,1600]{0,1:T(8,128)(2,1)}, u32[]{:S(2)}) %copy-start.1) | copy-done | bytes 3276824
  105.2 1.2 %convolution_bitcast_fusion.1 = f32[256,1024]{1,0:T(8,128)S(1)} fusion(bf16[8,256,200]{2,1,0:T(8,128)(2,1)S(1)} %bitcast.132, bf16[8,200,1024]{2,1,0:T(8,128)(2,1)S(1)} %bitcast.129), kind=kOutput, calls=%fused_computation.3 | convolution fusion | flops 838860800 | bytes 5144576 | tf_op jit(solution)/shard_map/ham,hmr->ar/dot_general | solution.py:172
  106.4 3.9 %fusion.1 = bf16[256,1024]{1,0:T(8,128)(2,1)} fusion(f32[256,1024]{1,0:T(8,128)S(1)} %convolution_bitcast_fusion.1, bf16[8,256,200]{2,1,0:T(8,128)(2,1)S(1)} %bitcast.131, bf16[8,200,1024]{2,1,0:T(8,128)(2,1)} %collective-permute-done.14), kind=kOutput, calls=%fused_computation.7 | convolution fusion | flops 839385088 | bytes 5668864 | tf_op jit(solution)/shard_map/ham,hmr->ar/dot_general | solution.py:172
  (54 shorter events, 1.4 us)
Async XLA Ops:
  0.0 2.0 %copy-start = (bf16[1024,512]{1,0:T(8,128)(2,1)S(1)}, bf16[1024,512]{1,0:T(8,128)(2,1)}, u32[]{:S(2)}) copy-start(bf16[1024,512]{1,0:T(8,128)(2,1)} %param.7) | copy-start | bytes 3145732
  2.5 3.8 %copy-start.2 = (f32[1600,400]{0,1:T(8,128)S(1)}, f32[1600,400]{0,1:T(8,128)}, u32[]{:S(2)}) copy-start(f32[1600,400]{0,1:T(8,128)} %param.9) | copy-start | bytes 7680004
  5.7 7.7 %collective-permute-start = (bf16[4,32,200]{2,1,0:T(8,128)(2,1)S(1)}, bf16[4,32,200]{2,1,0:T(8,128)(2,1)S(1)}, u32[]{:S(2)}, u32[]{:S(2)}) collective-permute-start(bf16[4,32,200]{2,1,0:T(8,128)(2,1)S(1)} %get-tuple-element.14), channel_id=1, source_target_pairs={{0,1},{1,0},{2,3},{3,2},{4,5},{5,4},{6,7},{7,6},{8,9},{9,8},{10,11... | collective-permute-start | bytes 153608 | tf_op jit(solution)/shard_map/ppermute | solution.py:103
  12.6 17.3 %collective-permute-start.1 = (bf16[4,400,200]{2,1,0:T(8,128)(2,1)}, bf16[4,400,200]{2,1,0:T(8,128)(2,1)}, u32[]{:S(2)}, u32[]{:S(2)}) collective-permute-start(bf16[4,400,200]{2,1,0:T(8,128)(2,1)} %select_bitcast_fusion), channel_id=1, source_target_pairs={{0,1},{1,0},{2,3},{3,2},{4,5},{5,4},{6,7},{7,6},{8,9},{9,8},{10,11... | collective-permute-start | bytes 1920008 | tf_op jit(solution)/shard_map/ppermute | solution.py:103
  14.1 14.7 %all-to-all-start = ((bf16[8,32,200]{2,1,0:T(8,128)(2,1)}), bf16[8,32,200]{2,1,0:T(8,128)(2,1)}, u32[]{:S(2)}, u32[]{:S(2)}) async-start(bf16[8,32,200]{2,1,0:T(8,128)(2,1)} %maximum_select_fusion.1), calls=%async_computation | async-start | bytes 262144 | tf_op jit(solution)/shard_map/all_to_all | solution.py:134
  29.8 2.2 %collective-permute-start.2 = (bf16[32,200]{1,0:T(8,128)(2,1)S(1)}, bf16[32,200]{1,0:T(8,128)(2,1)S(1)}, u32[]{:S(2)}, u32[]{:S(2)}) collective-permute-start(bf16[32,200]{1,0:T(8,128)(2,1)S(1)} %divide_convert_fusion.3), channel_id=1, source_target_pairs={{0,1},{1,0},{2,3},{3,2},{4,5},{5,4},{6,7},{7,6},{8,9},{9,8},{10,11... | collective-permute-start | bytes 38408 | tf_op jit(solution)/shard_map/ppermute | solution.py:103
  42.9 1.2 %collective-permute-start.3 = (bf16[32,200]{1,0:T(8,128)(2,1)S(1)}, bf16[32,200]{1,0:T(8,128)(2,1)S(1)}, u32[]{:S(2)}, u32[]{:S(2)}) collective-permute-start(bf16[32,200]{1,0:T(8,128)(2,1)S(1)} %divide_convert_fusion.2), channel_id=1, source_target_pairs={{0,1},{1,0},{2,3},{3,2},{4,5},{5,4},{6,7},{7,6},{8,9},{9,8},{10,11... | collective-permute-start | bytes 38408 | tf_op jit(solution)/shard_map/ppermute | solution.py:103
  54.7 1.2 %collective-permute-start.4 = (bf16[32,200]{1,0:T(8,128)(2,1)S(1)}, bf16[32,200]{1,0:T(8,128)(2,1)S(1)}, u32[]{:S(2)}, u32[]{:S(2)}) collective-permute-start(bf16[32,200]{1,0:T(8,128)(2,1)S(1)} %divide_convert_fusion.1), channel_id=1, source_target_pairs={{0,1},{1,0},{2,3},{3,2},{4,5},{5,4},{6,7},{7,6},{8,9},{9,8},{10,11... | collective-permute-start | bytes 38408 | tf_op jit(solution)/shard_map/ppermute | solution.py:103
  56.1 25.6 %copy-start.3 = (s32[16]{0:T(128)S(1)}, s32[16]{0:T(128)}, u32[]{:S(2)}) copy-start(s32[16]{0:T(128)} %param.11) | copy-start | bytes 196
  57.1 10.9 %all-to-all-start.3 = ((bf16[8,32,200]{2,1,0:T(8,128)(2,1)}), bf16[8,32,200]{2,1,0:T(8,128)(2,1)S(1)}, u32[]{:S(2)}, u32[]{:S(2)}) async-start(bf16[8,32,200]{2,1,0:T(8,128)(2,1)} %fusion.5), calls=%async_computation.3 | async-start | bytes 262144 | tf_op jit(solution)/shard_map/all_to_all | solution.py:134
  60.5 45.9 %collective-permute-start.14 = (bf16[8,200,1024]{2,1,0:T(8,128)(2,1)}, bf16[8,200,1024]{2,1,0:T(8,128)(2,1)}, u32[]{:S(2)}, u32[]{:S(2)}) collective-permute-start(bf16[8,200,1024]{2,1,0:T(8,128)(2,1)} %bitcast.128), channel_id=1, source_target_pairs={{0,1},{1,0},{2,3},{3,2},{4,5},{5,4},{6,7},{7,6},{8,9},{9,8},{10,11... | collective-permute-start | bytes 9830408 | tf_op jit(solution)/shard_map/ppermute | solution.py:103
  68.0 1.2 %collective-permute-start.5 = (bf16[32,200]{1,0:T(8,128)(2,1)S(1)}, bf16[32,200]{1,0:T(8,128)(2,1)S(1)}, u32[]{:S(2)}, u32[]{:S(2)}) collective-permute-start(bf16[32,200]{1,0:T(8,128)(2,1)S(1)} %divide_convert_fusion), channel_id=1, source_target_pairs={{0,1},{1,0},{2,3},{3,2},{4,5},{5,4},{6,7},{7,6},{8,9},{9,8},{10,11... | collective-permute-start | bytes 38408 | tf_op jit(solution)/shard_map/ppermute | solution.py:103
  70.4 10.9 %all-to-all-start.4 = ((bf16[8,32,200]{2,1,0:T(8,128)(2,1)}), bf16[8,32,200]{2,1,0:T(8,128)(2,1)S(1)}, u32[]{:S(2)}, u32[]{:S(2)}) async-start(bf16[8,32,200]{2,1,0:T(8,128)(2,1)} %fusion.6), calls=%async_computation.4 | async-start | bytes 262144 | tf_op jit(solution)/shard_map/all_to_all | solution.py:134
  81.4 5.2 %collective-permute-start.6 = (bf16[1,32,200]{2,1,0:T(8,128)(2,1)S(1)}, bf16[1,32,200]{2,1,0:T(8,128)(2,1)S(1)}, u32[]{:S(2)}, u32[]{:S(2)}) collective-permute-start(bf16[1,32,200]{2,1,0:T(8,128)(2,1)S(1)} %get-tuple-element.6), channel_id=1, source_target_pairs={{0,2},{2,0},{4,6},{6,4},{8,10},{10,8},{12,14},{14,12},{1,3},{3,1},... | collective-permute-start | bytes 38408 | tf_op jit(solution)/shard_map/ppermute | solution.py:160
  82.0 16.1 %collective-permute-start.11 = (bf16[1,32,200]{2,1,0:T(8,128)(2,1)S(1)}, bf16[1,32,200]{2,1,0:T(8,128)(2,1)S(1)}, u32[]{:S(2)}, u32[]{:S(2)}) collective-permute-start(bf16[1,32,200]{2,1,0:T(8,128)(2,1)S(1)} %get-tuple-element.6), channel_id=1, source_target_pairs={{0,12},{2,14},{4,8},{6,10},{8,4},{10,6},{12,0},{14,2},{1,13},{3,15... | collective-permute-start | bytes 38408 | tf_op jit(solution)/shard_map/ppermute | solution.py:160
  83.7 14.4 %collective-permute-start.10 = (bf16[1,32,200]{2,1,0:T(8,128)(2,1)S(1)}, bf16[1,32,200]{2,1,0:T(8,128)(2,1)S(1)}, u32[]{:S(2)}, u32[]{:S(2)}) collective-permute-start(bf16[1,32,200]{2,1,0:T(8,128)(2,1)S(1)} %get-tuple-element.6), channel_id=1, source_target_pairs={{0,10},{2,8},{4,14},{6,12},{8,2},{10,0},{12,6},{14,4},{1,11},{3,9}... | collective-permute-start | bytes 38408 | tf_op jit(solution)/shard_map/ppermute | solution.py:160
  84.6 13.5 %collective-permute-start.9 = (bf16[1,32,200]{2,1,0:T(8,128)(2,1)S(1)}, bf16[1,32,200]{2,1,0:T(8,128)(2,1)S(1)}, u32[]{:S(2)}, u32[]{:S(2)}) collective-permute-start(bf16[1,32,200]{2,1,0:T(8,128)(2,1)S(1)} %get-tuple-element.6), channel_id=1, source_target_pairs={{0,8},{2,10},{4,12},{6,14},{8,0},{10,2},{12,4},{14,6},{1,9},{3,11}... | collective-permute-start | bytes 38408 | tf_op jit(solution)/shard_map/ppermute | solution.py:160
  86.6 3.7 %collective-permute-start.7 = (bf16[1,32,200]{2,1,0:T(8,128)(2,1)S(1)}, bf16[1,32,200]{2,1,0:T(8,128)(2,1)S(1)}, u32[]{:S(2)}, u32[]{:S(2)}) collective-permute-start(bf16[1,32,200]{2,1,0:T(8,128)(2,1)S(1)} %get-tuple-element.6), channel_id=1, source_target_pairs={{0,4},{2,6},{4,0},{6,2},{8,12},{10,14},{12,8},{14,10},{1,5},{3,7},... | collective-permute-start | bytes 38408 | tf_op jit(solution)/shard_map/ppermute | solution.py:160
  90.3 4.6 %collective-permute-start.8 = (bf16[1,32,200]{2,1,0:T(8,128)(2,1)S(1)}, bf16[1,32,200]{2,1,0:T(8,128)(2,1)S(1)}, u32[]{:S(2)}, u32[]{:S(2)}) collective-permute-start(bf16[1,32,200]{2,1,0:T(8,128)(2,1)S(1)} %get-tuple-element.6), channel_id=1, source_target_pairs={{0,6},{2,4},{4,2},{6,0},{8,14},{10,12},{12,10},{14,8},{1,7},{3,5},... | collective-permute-start | bytes 38408 | tf_op jit(solution)/shard_map/ppermute | solution.py:160
  95.0 6.4 %collective-permute-start.12 = (bf16[1,32,200]{2,1,0:T(8,128)(2,1)S(1)}, bf16[1,32,200]{2,1,0:T(8,128)(2,1)S(1)}, u32[]{:S(2)}, u32[]{:S(2)}) collective-permute-start(bf16[1,32,200]{2,1,0:T(8,128)(2,1)S(1)} %get-tuple-element.6), channel_id=1, source_target_pairs={{0,14},{2,12},{4,10},{6,8},{8,6},{10,4},{12,2},{14,0},{1,15},{3,13... | collective-permute-start | bytes 38408 | tf_op jit(solution)/shard_map/ppermute | solution.py:160
  101.4 1.3 %collective-permute-start.13 = (bf16[8,32,200]{2,1,0:T(8,128)(2,1)S(1)}, bf16[8,32,200]{2,1,0:T(8,128)(2,1)S(1)}, u32[]{:S(2)}, u32[]{:S(2)}) collective-permute-start(bf16[8,32,200]{2,1,0:T(8,128)(2,1)S(1)} %constant_dynamic-update-slice_fusion), channel_id=1, source_target_pairs={{0,1},{1,0},{2,3},{3,2},{4,5},{5,4},{6,7},{7,6},{8,9},{9,8},{10,11... | collective-permute-start | bytes 307208 | tf_op jit(solution)/shard_map/ppermute | solution.py:103
  103.3 1.9 %copy-start.1 = (bf16[1024,1600]{0,1:T(8,128)(2,1)S(1)}, bf16[1024,1600]{0,1:T(8,128)(2,1)}, u32[]{:S(2)}) copy-start(bf16[1024,1600]{0,1:T(8,128)(2,1)} %param.6) | copy-start | bytes 9830404
